TPU v7x, 32 devices: a whole 2x2x4 slice. The times are simulated.
32 devices in a mesh: dp: 2 (over x), fsdp: 16 (over z, y, core).
Axes of the slice: x: 2, y: 2, z: 4, core: 2. Of those that a mesh axis runs over, the one named last changes fastest.
Arguments:
- tokens: bfloat16 [18432, 768], P(('dp', 'fsdp')), may hold values from -6 to 6
- gain_attn: bfloat16 [768], P(('dp', 'fsdp')), may hold values from 0.25 to 1.75
- w_qkv: bfloat16 [768, 2304], P(('dp', 'fsdp')), may hold values from -0.21875 to 0.21875
- w_proj: bfloat16 [768, 768], P(('dp', 'fsdp')), may hold values from -2.5 to 2.5
- gain_moe: bfloat16 [768], P(('dp', 'fsdp')), may hold values from 0.25 to 1.75
- w_router: bfloat16 [768, 8], P(('dp', 'fsdp')), may hold values from -0.15625 to 0.15625
- w_in: bfloat16 [8, 768, 3072], P('dp', 'fsdp'), may hold values from -0.21875 to 0.21875
- w_out: bfloat16 [8, 3072, 768], P('dp', 'fsdp'), may hold values from -0.875 to 0.875
- routes: int32 [18432, 2], P(('dp', 'fsdp')), may hold values from 0 to 7, as said below
- slot_ids: int32 [18432, 2], P(('dp', 'fsdp')), may hold values from 0 to 152, as said below
- cotangent: bfloat16 [18432, 768], P(('dp', 'fsdp')), may hold values from -6 to 6
Outputs:
- output: bfloat16 [18432, 768], P(('dp', 'fsdp'))
- grad_tokens: float32 [18432, 768], P(('dp', 'fsdp'))
- d_gain_attn: float32 [768], P(('dp', 'fsdp'))
- d_qkv: float32 [768, 2304], P(('dp', 'fsdp'))
- d_proj: float32 [768, 768], P(('dp', 'fsdp'))
- d_gain_moe: float32 [768], P(('dp', 'fsdp'))
- d_router: float32 [768, 8], P(('dp', 'fsdp'))
- d_in: float32 [8, 768, 3072], P('dp', 'fsdp')
- d_out: float32 [8, 3072, 768], P('dp', 'fsdp')
Inputs may be any that keep to these rules, and one draw needn't show every extreme that they name: `routes`: each row names two different experts. `slot_ids`: among the 576 patches of one device, the pairs routed to one expert hold the distinct slots 0, 1, 2, ... in some priority order; a pair beyond the 152 slots holds 152 and is dropped. On every device some expert gets more than 152 pairs.
All inputs are finite; a program needn't handle non-finite values.
Results may differ from a plain program's by a relative error of at most 0.017.
Values may be sent and summed in bfloat16 or wider, within the bound.
No kernel may reach another device: no remote copies, remote signals or barrier semaphores. Data moves between devices by JAX's collectives and lax.ppermute only.
A program may use at most 320 MiB of HBM per device.

v0:
```python
import jax
import jax.numpy as jnp
from jax import lax
from jax.sharding import PartitionSpec as P

HEADS = 12
HEAD_DIM = 64
EXPERTS = 8
SEQ = 576
CAP = 152
norm_epsilon = 1e-06


def norm_parts(values):
    centre = values - jnp.mean(values, axis=-1, keepdims=True)
    inverse = lax.rsqrt(jnp.mean(centre * centre, axis=-1, keepdims=True) + norm_epsilon)
    return (centre * inverse, inverse)


def norm_back(grad_normed, normed, inverse):
    mean_grad = jnp.mean(grad_normed, axis=-1, keepdims=True)
    mean_cross = jnp.mean(grad_normed * normed, axis=-1, keepdims=True)
    return (grad_normed - mean_grad - normed * mean_cross) * inverse


def gelu_tanh(values):
    return jax.nn.gelu(values, approximate=True)


def head_forward(operands):
    queries, keys_head, values_head = operands
    scores = jnp.einsum(
        "isd,itd->ist", queries, keys_head, preferred_element_type=jnp.float32
    ) * HEAD_DIM ** (-0.5)
    largest = jnp.max(scores, axis=-1, keepdims=True)
    powers = jnp.exp(scores - largest)
    totals = jnp.sum(powers, axis=-1, keepdims=True)
    attn_probs = (powers / totals).astype(jnp.bfloat16)
    head_out = jnp.einsum(
        "ist,itd->isd", attn_probs, values_head, preferred_element_type=jnp.float32
    )
    return (head_out.astype(jnp.bfloat16), (largest + jnp.log(totals))[..., 0])


def head_backward(operands):
    queries, keys_head, values_head, grad_head, log_total = operands
    scores = jnp.einsum(
        "isd,itd->ist", queries, keys_head, preferred_element_type=jnp.float32
    ) * HEAD_DIM ** (-0.5)
    attn_probs = jnp.exp(scores - log_total[..., None])
    grad_probs = jnp.einsum(
        "isd,itd->ist", grad_head, values_head, preferred_element_type=jnp.float32
    )
    row_terms = jnp.sum(attn_probs * grad_probs, axis=-1, keepdims=True)
    grad_scores = (attn_probs * (grad_probs - row_terms)).astype(jnp.bfloat16)
    grad_query = jnp.einsum(
        "ist,itd->isd", grad_scores, keys_head, preferred_element_type=jnp.float32
    ) * HEAD_DIM ** (-0.5)
    grad_key = jnp.einsum(
        "ist,isd->itd", grad_scores, queries, preferred_element_type=jnp.float32
    ) * HEAD_DIM ** (-0.5)
    grad_value = jnp.einsum(
        "ist,isd->itd",
        attn_probs.astype(jnp.bfloat16),
        grad_head,
        preferred_element_type=jnp.float32,
    )
    return (grad_query, grad_key, grad_value)


def expert_forward(expert_rows, w_up, w_down):
    pre_act = jnp.einsum("ecd,edf->ecf", expert_rows, w_up, preferred_element_type=jnp.float32)
    hidden = gelu_tanh(pre_act).astype(jnp.bfloat16)
    result = jnp.einsum("ecf,efd->ecd", hidden, w_down, preferred_element_type=jnp.float32).astype(
        jnp.bfloat16
    )
    return (pre_act, hidden, result)


def expert_backward(expert_rows, pre_act, hidden, grad_result, w_up, w_down):
    grad_hidden = jnp.einsum(
        "ecd,efd->ecf", grad_result, w_down, preferred_element_type=jnp.float32
    )
    ignored, pull_back = jax.vjp(gelu_tanh, pre_act)
    grad_pre = pull_back(grad_hidden)[0].astype(jnp.bfloat16)
    grad_down = jnp.einsum("ecf,ecd->efd", hidden, grad_result, preferred_element_type=jnp.float32)
    grad_up = jnp.einsum("ecd,ecf->edf", expert_rows, grad_pre, preferred_element_type=jnp.float32)
    grad_rows = jnp.einsum(
        "ecf,edf->ecd", grad_pre, w_up, preferred_element_type=jnp.float32
    ).astype(jnp.bfloat16)
    return (grad_up, grad_down, grad_rows)


def gather_dense(gain_attn, w_qkv, w_proj, gain_moe, w_router):
    return (
        lax.all_gather(gain_attn, ("dp", "fsdp"), axis=0, tiled=True),
        lax.all_gather(w_qkv, ("dp", "fsdp"), axis=0, tiled=True),
        lax.all_gather(w_proj, ("dp", "fsdp"), axis=0, tiled=True),
        lax.all_gather(gain_moe, ("dp", "fsdp"), axis=0, tiled=True),
        lax.all_gather(w_router, ("dp", "fsdp"), axis=0, tiled=True),
    )


def gather_experts(w_in, w_out):
    local_pair = (w_in, w_out)
    return (
        lax.all_gather(local_pair[0], "fsdp", axis=1, tiled=True),
        lax.all_gather(local_pair[1], "fsdp", axis=1, tiled=True),
    )


def reduce_experts(grad_up, grad_down):
    reduced = (
        lax.psum_scatter(
            grad_up.astype(jnp.bfloat16), "fsdp", scatter_dimension=1, tiled=True
        ).astype(jnp.float32),
        lax.psum_scatter(
            grad_down.astype(jnp.bfloat16), "fsdp", scatter_dimension=1, tiled=True
        ).astype(jnp.float32),
    )
    return reduced


def per_device(
    tokens, gain_attn, w_qkv, w_proj, gain_moe, w_router, w_in, w_out, routes, slot_ids, cotangent
):
    dense_full = gather_dense(gain_attn, w_qkv, w_proj, gain_moe, w_router)
    expert_weights = gather_experts(w_in, w_out)
    rows_here = tokens.shape[0]
    images = rows_here // SEQ
    residual = tokens.astype(jnp.float32)
    normed_one, inverse_one = norm_parts(residual)
    gain_one = dense_full[0].astype(jnp.float32)
    act_one = (normed_one * gain_one).astype(jnp.bfloat16)
    qkv = jnp.dot(act_one, dense_full[1], preferred_element_type=jnp.float32).astype(jnp.bfloat16)
    split_qkv = qkv.reshape(images, SEQ, 3, HEADS, HEAD_DIM).transpose(2, 3, 0, 1, 4)
    head_out, head_lse = lax.map(head_forward, (split_qkv[0], split_qkv[1], split_qkv[2]))
    attended = head_out.transpose(1, 2, 0, 3).reshape(rows_here, -1)
    resid_mid = residual + jnp.dot(attended, dense_full[2], preferred_element_type=jnp.float32)
    normed_two, inverse_two = norm_parts(resid_mid)
    gain_two = dense_full[3].astype(jnp.float32)
    act_two = (normed_two * gain_two).astype(jnp.bfloat16)
    logits = jnp.dot(act_two, dense_full[4], preferred_element_type=jnp.float32)
    router = jax.nn.softmax(logits, axis=-1)
    expert_ids = lax.broadcasted_iota(jnp.int32, (1, 1, EXPERTS), 2)
    chosen = routes[:, :, None] == expert_ids
    gate_values = jnp.sum(jnp.where(chosen, router[:, None, :], 0.0), axis=-1)
    gates_low = gate_values.astype(jnp.bfloat16)
    slot_count = EXPERTS * CAP
    columns = lax.broadcasted_iota(jnp.int32, (1, 1, slot_count), 2)
    live_pair = slot_ids < CAP
    targets = routes * CAP + slot_ids
    matches = (targets[:, :, None] == columns) & live_pair[:, :, None]
    dispatch = jnp.sum(matches.astype(jnp.bfloat16), axis=1)
    combine = jnp.sum(
        jnp.where(matches, gates_low[:, :, None], jnp.zeros((), jnp.bfloat16)), axis=1
    )
    slot_rows = (
        jnp.einsum("tx,td->xd", dispatch, act_two, preferred_element_type=jnp.float32)
        .astype(jnp.bfloat16)
        .reshape(EXPERTS, CAP, -1)
    )
    expert_rows = lax.all_to_all(slot_rows, "dp", split_axis=0, concat_axis=1, tiled=True)
    pre_act, hidden, result = expert_forward(expert_rows, expert_weights[0], expert_weights[1])
    slot_result = lax.all_to_all(result, "dp", split_axis=1, concat_axis=0, tiled=True)
    flat_result = slot_result.reshape(slot_count, -1)
    moe_sum = jnp.einsum("tx,xd->td", combine, flat_result, preferred_element_type=jnp.float32)
    output = (resid_mid + moe_sum).astype(jnp.bfloat16)
    dense_full = gather_dense(gain_attn, w_qkv, w_proj, gain_moe, w_router)
    expert_weights = gather_experts(w_in, w_out)
    grad_slots = (
        jnp.einsum("tx,td->xd", combine, cotangent, preferred_element_type=jnp.float32)
        .astype(jnp.bfloat16)
        .reshape(EXPERTS, CAP, -1)
    )
    picked = flat_result[jnp.clip(targets, 0, slot_count - 1)]
    grad_gates = jnp.where(
        live_pair,
        jnp.einsum("tkd,td->tk", picked, cotangent, preferred_element_type=jnp.float32),
        0.0,
    )
    grad_router = jnp.sum(jnp.where(chosen, grad_gates[:, :, None], 0.0), axis=1)
    grad_logits = (
        router * (grad_router - jnp.sum(router * grad_router, axis=-1, keepdims=True))
    ).astype(jnp.bfloat16)
    d_router = jnp.einsum("td,te->de", act_two, grad_logits, preferred_element_type=jnp.float32)
    grad_act_two = jnp.einsum(
        "te,de->td", grad_logits, dense_full[4], preferred_element_type=jnp.float32
    )
    grad_expert = lax.all_to_all(grad_slots, "dp", split_axis=0, concat_axis=1, tiled=True)
    grad_up, grad_down, grad_rows = expert_backward(
        expert_rows, pre_act, hidden, grad_expert, expert_weights[0], expert_weights[1]
    )
    grad_rows = lax.all_to_all(grad_rows, "dp", split_axis=1, concat_axis=0, tiled=True)
    grad_act_two = grad_act_two + jnp.einsum(
        "tx,xd->td", dispatch, grad_rows.reshape(slot_count, -1), preferred_element_type=jnp.float32
    )
    d_gain_moe = jnp.sum(grad_act_two * normed_two, axis=0)
    grad_mid = cotangent.astype(jnp.float32) + norm_back(
        grad_act_two * gain_two, normed_two, inverse_two
    )
    grad_mid_low = grad_mid.astype(jnp.bfloat16)
    d_proj = jnp.einsum("td,te->de", attended, grad_mid_low, preferred_element_type=jnp.float32)
    grad_attended = jnp.einsum(
        "te,de->td", grad_mid_low, dense_full[2], preferred_element_type=jnp.float32
    ).astype(jnp.bfloat16)
    grad_heads = grad_attended.reshape(images, SEQ, HEADS, HEAD_DIM).transpose(2, 0, 1, 3)
    grad_query, grad_key, grad_value = lax.map(
        head_backward, (split_qkv[0], split_qkv[1], split_qkv[2], grad_heads, head_lse)
    )
    grad_qkv = (
        jnp.stack([grad_query, grad_key, grad_value])
        .transpose(2, 3, 0, 1, 4)
        .reshape(rows_here, -1)
        .astype(jnp.bfloat16)
    )
    d_qkv = jnp.einsum("td,te->de", act_one, grad_qkv, preferred_element_type=jnp.float32)
    grad_act_one = jnp.einsum(
        "te,de->td", grad_qkv, dense_full[1], preferred_element_type=jnp.float32
    )
    d_gain_attn = jnp.sum(grad_act_one * normed_one, axis=0)
    grad_tokens = grad_mid + norm_back(grad_act_one * gain_one, normed_one, inverse_one)
    dense_grads = (
        lax.psum_scatter(d_gain_attn, ("dp", "fsdp"), scatter_dimension=0, tiled=True),
        lax.psum_scatter(d_qkv, ("dp", "fsdp"), scatter_dimension=0, tiled=True),
        lax.psum_scatter(d_proj, ("dp", "fsdp"), scatter_dimension=0, tiled=True),
        lax.psum_scatter(d_gain_moe, ("dp", "fsdp"), scatter_dimension=0, tiled=True),
        lax.psum_scatter(d_router, ("dp", "fsdp"), scatter_dimension=0, tiled=True),
    )
    expert_grads = reduce_experts(grad_up, grad_down)
    return (
        output,
        grad_tokens,
        dense_grads[0],
        dense_grads[1],
        dense_grads[2],
        dense_grads[3],
        dense_grads[4],
        expert_grads[0],
        expert_grads[1],
    )


def solution(mesh):
    in_specs = (
        P(("dp", "fsdp"), None),
        P(("dp", "fsdp")),
        P(("dp", "fsdp"), None),
        P(("dp", "fsdp"), None),
        P(("dp", "fsdp")),
        P(("dp", "fsdp"), None),
        P("dp", "fsdp", None),
        P("dp", "fsdp", None),
        P(("dp", "fsdp"), None),
        P(("dp", "fsdp"), None),
        P(("dp", "fsdp"), None),
    )
    out_specs = (
        P(("dp", "fsdp"), None),
        P(("dp", "fsdp"), None),
        P(("dp", "fsdp")),
        P(("dp", "fsdp"), None),
        P(("dp", "fsdp"), None),
        P(("dp", "fsdp")),
        P(("dp", "fsdp"), None),
        P("dp", "fsdp", None),
        P("dp", "fsdp", None),
    )
    return jax.shard_map(
        per_device, mesh=mesh, in_specs=in_specs, out_specs=out_specs, check_vma=False
    )
```

profile of v0, /device:TPU:0, one launch (start us, length us, event | category | flops | bytes accessed | tf_op | source)
XLA Modules:
  0.0 1001.7 jit_solution(7998535637937780949)
XLA Ops:
  10.6 42.0 %all-reduce.6 = (bf16[768]{0:T(1024)(128)(2,1)S(1)}, bf16[768]{0:T(1024)(128)(2,1)S(1)}) all-reduce(bf16[768]{0:T(1024)(128)(2,1)S(1)} %dynamic-update-slice, bf16[768]{0:T(1024)(128)(2,1)S(1)} %dynamic-update-slice.1), channel_id=1, replica_groups=mesh['dp'=2,'fsdp'=16] {'dp','fsdp'}, use_global_device_ids=true, to_apply=%add | all-reduce | flops 1536 | bytes 6144
  52.6 40.8 %all-gather = bf16[32,24,8]{1,2,0:T(8,128)(2,1)S(1)} all-gather(bf16[1,24,8]{1,2,0:T(8,128)(2,1)S(1)} %bitcast.199), channel_id=1, replica_groups=mesh['dp'=2,'fsdp'=16] {'dp','fsdp'}, dimensions={0}, use_global_device_ids=true | all-gather | bytes 12672 | tf_op jit(solution)/shard_map/all_gather | solution.py:100
  95.4 5.9 convolution_convert_fusion.3
  101.3 4.0 copy.102
  110.8 2.6 copy.105
  113.4 37.9 %while.26 = (s32[]{:T(128)}, bf16[12,1,576,64]{2,3,1,0:T(8,128)(2,1)}, f32[12,1,576]{2,1,0:T(1,128)}, bf16[12,1,576,64]{3,2,1,0:T(8,128)(2,1)S(1)}, bf16[12,1,57...) while((s32[]{:T(128)}, bf16[12,1,576,64]{2,3,1,0:T(8,128)(2,1)}, ...), condition=%wide.region_5.6_spmd, body=%wide.region_2.5_spmd.sunk | while | flops 87293376 | bytes 4531033 | solution.py:137
  114.0 1.9 fusion.134
  117.1 1.9 fusion.134
  120.3 1.9 fusion.134
  123.4 1.9 fusion.134
  126.6 1.9 fusion.134
  129.7 1.9 fusion.134
  132.8 1.9 fusion.134
  136.0 2.0 fusion.134
  139.2 1.9 fusion.134
  142.3 2.0 fusion.134
  145.5 2.0 fusion.134
  148.7 2.0 fusion.134
  151.3 4.1 fusion.75
  157.2 3.7 fusion.48
  160.9 2.9 convolution_convert_fusion.4
  163.8 3.7 all-to-all-start.2
  167.5 4.4 convolution_convert_fusion.5
  171.9 18.5 %all-to-all-done.2 = bf16[8,152,768]{2,1,0:T(8,128)(2,1)S(1)} async-done(((bf16[8,152,768]{2,1,0:T(8,128)(2,1)}), bf16[8,152,768]{2,1,0:T(8,128)(2,1)S(1)}, u32[]{:S(2)}, u32[]{:S(2)}) %all-to-all-start.2) | async-done | bytes 1867808 | tf_op jit(solution)/shard_map/all_to_all | solution.py:190
  191.7 4.8 all-to-all-start
  198.6 20.2 %all-to-all-done = bf16[8,152,768]{2,1,0:T(8,128)(2,1)} async-done(((bf16[8,152,768]{2,1,0:T(8,128)(2,1)}), bf16[8,152,768]{2,1,0:T(8,128)(2,1)}, u32[]{:S(2)}, u32[]{:S(2)}) %all-to-all-start) | async-done | bytes 1867808 | tf_op jit(solution)/shard_map/all_to_all | solution.py:163
  218.8 2.9 copy.107
  221.7 7.1 all-gather.12.cloned.1.call-done
  228.8 12.9 %fusion.77 = f32[4,304,3072]{2,1,0:T(8,128)} fusion(bf16[4,304,768]{2,1,0:T(8,128)(2,1)S(1)} %bitcast.182, bf16[4,3072,768]{2,1,0:T(8,128)(2,1)} %all-gather.12.cloned.1.call-done), kind=kOutput, calls=%fused_computation.141 | convolution fusion | flops 5737807872 | bytes 35684352 | tf_op jit(solution)/shard_map/ecd,efd->ecf/dot_general | solution.py:81
  241.7 87.4 %all-gather.10.cloned.1.call-done = bf16[4,768,3072]{2,1,0:T(8,128)(2,1)} async-done(((bf16[4,48,3072]{2,1,0:T(8,128)(2,1)}), bf16[4,768,3072]{2,1,0:T(8,128)(2,1)}) %all-gather.10.cloned.1.call-update) | async-done | bytes 18874384 | tf_op jit(solution)/shard_map/all_gather | solution.py:107
  329.1 26.9 %fusion.43 = (bf16[4,304,3072]{2,1,0:T(8,128)(2,1)}, f32[4,304,3072]{2,1,0:T(8,128)}) fusion(f32[4,304,3072]{2,1,0:T(8,128)} %fusion.77, bf16[4,304,768]{2,1,0:T(8,128)(2,1)} %bitcast.192, bf16[4,768,3072]{2,1,0:T(8,128)(2,1)} %all-gather.10.cloned.1.call-done), kind=kOutput, calls=%fused_computation.59 | convolution fusion | flops 5812518912 | bytes 58097664 | tf_op jit(solution)/shard_map/ecd,edf->ecf/dot_general | solution.py:72
  356.0 16.5 %convolution_convert_fusion.2 = bf16[4,768,3072]{2,1,0:T(8,128)(2,1)} fusion(bf16[4,304,768]{2,1,0:T(8,128)(2,1)} %bitcast.193, bf16[4,304,3072]{2,1,0:T(8,128)(2,1)} %get-tuple-element.212), kind=kOutput, calls=%fused_computation.62 | convolution fusion | flops 5747245056 | bytes 28213248 | tf_op jit(solution)/shard_map/ecd,ecf->edf/dot_general | solution.py:87
  372.8 20.0 %convolution_convert_fusion.1 = bf16[4,3072,768]{2,1,0:T(8,128)(2,1)} fusion(bf16[4,304,768]{2,1,0:T(8,128)(2,1)S(1)} %bitcast.183, f32[4,304,3072]{2,1,0:T(8,128)} %get-tuple-element.213), kind=kOutput, calls=%fused_computation.61 | convolution fusion | flops 5780865024 | bytes 35684352 | tf_op jit(solution)/shard_map/ecf,ecd->efd/dot_general | solution.py:86
  392.9 19.3 %convolution_convert_fusion.7 = bf16[4,304,768]{2,1,0:T(8,128)(2,1)S(1)} fusion(bf16[4,3072,768]{2,1,0:T(8,128)(2,1)} %all-gather.12.cloned.1.call-done, f32[4,304,3072]{2,1,0:T(8,128)} %get-tuple-element.213), kind=kOutput, calls=%fused_computation.85 | convolution fusion | flops 5772361728 | bytes 35684352 | tf_op jit(solution)/shard_map/ecf,efd->ecd/dot_general | solution.py:74
  412.2 2.2 copy.108
  414.4 3.9 all-to-all-start.1
  418.4 13.2 %convolution_convert_fusion.6 = bf16[4,304,768]{2,1,0:T(8,128)(2,1)} fusion(bf16[4,304,3072]{2,1,0:T(8,128)(2,1)} %get-tuple-element.212, bf16[4,768,3072]{2,1,0:T(8,128)(2,1)} %all-gather.10.cloned.1.call-done), kind=kOutput, calls=%fused_computation.84 | convolution fusion | flops 5738741760 | bytes 28213248 | tf_op jit(solution)/shard_map/ecf,edf->ecd/dot_general | solution.py:88
  431.6 3.7 copy.112
  435.3 6.1 all-to-all-done.1
  442.6 4.8 all-to-all-start.3
  449.7 20.1 %all-to-all-done.3 = bf16[4,304,768]{2,0,1:T(4,128)(2,1)} async-done(((bf16[4,304,768]{2,0,1:T(4,128)(2,1)}), bf16[4,304,768]{2,0,1:T(4,128)(2,1)}, u32[]{:S(2)}, u32[]{:S(2)}) %all-to-all-start.3) | async-done | bytes 1867808 | tf_op jit(solution)/shard_map/all_to_all | solution.py:194
  472.9 4.8 gather_fusion
  477.7 4.7 reshape.217
  482.4 6.0 fusion.62
  489.7 3.0 fusion.78
  499.1 4.3 fusion.66
  503.7 100.7 %while.27 = (s32[]{:T(128)}, bf16[12,1,576,64]{2,3,1,0:T(8,128)(2,1)}, bf16[12,1,576,64]{2,3,1,0:T(8,128)(2,1)}, bf16[12,1,576,64]{2,3,1,0:T(8,128)(2,1)}, bf16[...) while((s32[]{:T(128)}, ...), condition=%wide.region_19.20_spmd, body=%wide.region_17.19_spmd.sunk | while | flops 215064000 | bytes 11510129 | solution.py:208
  524.0 1.9 fusion.144
  534.2 1.9 fusion.145
  550.9 1.9 fusion.145
  575.9 1.9 fusion.145
  584.4 2.0 fusion.145
  593.0 1.9 fusion.145
  601.5 1.9 fusion.145
  608.4 5.5 fusion.71
  615.2 7.2 fusion.60
  622.4 43.2 %all-reduce.5 = (f32[768]{0:T(1024)S(1)}, f32[768]{0:T(1024)S(1)}, f32[768,8]{0,1:T(8,128)S(1)}) all-reduce(f32[768]{0:T(1024)S(1)} %get-tuple-element.158, f32[768]{0:T(1024)S(1)} %get-tuple-element.156, f32[768,8]{0,1:T(8,128)S(1)} %fusion.79), channel_id=2, replica_groups=mesh['dp'=2,'fsdp'=16] {'dp','fsdp'}, use_global_device_ids=true, to_apply=%region_23.24.clone | all-reduce | flops 7680 | bytes 61440
  667.4 4.0 fusion.59
  671.4 2.2 add_convert_fusion
  673.7 3.0 convert_element_type.122
  676.7 88.2 %reduce-scatter.12.cloned.1.call-done = bf16[4,192,768]{2,1,0:T(8,128)(2,1)} async-done(((bf16[4,3072,768]{2,1,0:T(8,128)(2,1)}), bf16[4,192,768]{2,1,0:T(8,128)(2,1)}) %reduce-scatter.12.cloned.1.call-update) | async-done | bytes 1179664 | tf_op jit(solution)/shard_map/reduce_scatter | solution.py:117
  764.9 2.9 convert_element_type.124
  767.8 101.8 %reduce-scatter.8.cloned.1.call-done = f32[24,768]{1,0:T(8,128)} async-done(((f32[768,768]{1,0:T(8,128)}), f32[24,768]{1,0:T(8,128)}) %reduce-scatter.8.cloned.1.call-update) | async-done | bytes 73744 | tf_op jit(solution)/shard_map/reduce_scatter | solution.py:226
  869.6 124.8 %reduce-scatter.6.cloned.1.call-done = f32[24,2304]{1,0:T(8,128)} async-done(((f32[768,2304]{1,0:T(8,128)}), f32[24,2304]{1,0:T(8,128)}) %reduce-scatter.6.cloned.1.call-update) | async-done | bytes 221200 | tf_op jit(solution)/shard_map/reduce_scatter | solution.py:225
  (276 shorter events, 138.9 us)
Async XLA Ops:
  7.2 2.9 copy-start.36
  7.2 3.1 copy-start.37
  7.2 45.4 %copy-start.34 = (bf16[24,8]{0,1:T(8,128)(2,1)S(1)}, bf16[24,8]{0,1:T(8,128)(2,1)}, u32[]{:S(2)}) copy-start(bf16[24,8]{0,1:T(8,128)(2,1)} %param.20) | copy-start | bytes 1156
  7.2 86.3 %copy-start.8 = (bf16[576,768]{1,0:T(8,128)(2,1)S(1)}, bf16[576,768]{1,0:T(8,128)(2,1)}, u32[]{:S(2)}) copy-start(bf16[576,768]{1,0:T(8,128)(2,1)} %param.15) | copy-start | bytes 2654212
  7.2 88.2 %all-gather.6.cloned.1.call-start = ((), (), s32[]{:S(2)}) async-start(), calls=%async_computation.8 | async-start | bytes 3649536 | tf_op jit(solution)/shard_map/all_gather | solution.py:97
  8.0 143.4 %all-gather.8.cloned.1.call-start = ((), (), s32[]{:S(2)}) async-start(), calls=%async_computation.9 | async-start | bytes 1216512 | tf_op jit(solution)/shard_map/all_gather | solution.py:98
  8.7 220.1 %all-gather.12.cloned.1.call-start = ((), (), s32[]{:S(2)}) async-start(), calls=%async_computation.11 | async-start | bytes 20054016 | tf_op jit(solution)/shard_map/all_gather | solution.py:108
  9.4 84.7 %copy-start.21 = (s32[576,2]{0,1:T(2,128)S(1)}, s32[576,2]{0,1:T(2,128)}, u32[]{:S(2)}) copy-start(s32[576,2]{0,1:T(2,128)} %param.24) | copy-start | bytes 13828
  9.4 85.3 %copy-start.23 = (s32[576,2]{0,1:T(2,128)S(1)}, s32[576,2]{0,1:T(2,128)}, u32[]{:S(2)}) copy-start(s32[576,2]{0,1:T(2,128)} %param.23) | copy-start | bytes 13828
  9.5 319.6 %all-gather.10.cloned.1.call-start = ((), (), s32[]{:S(2)}) async-start(), calls=%async_computation.10 | async-start | bytes 20054016 | tf_op jit(solution)/shard_map/all_gather | solution.py:107
  52.6 42.8 %copy-start.29 = (f32[768]{0:T(1024)}, f32[768]{0:T(1024)S(1)}, u32[]{:S(2)}) copy-start(f32[768]{0:T(1024)S(1)} %convert_element_type.101) | copy-start | bytes 9220
  93.7 1.6 copy-start.25
  94.8 0.6 copy-start.31
  151.3 4.1 copy-start.4
  151.3 4.2 copy-start.5
  155.5 1.2 copy-start
  155.9 1.2 copy-start.24
  155.9 1.3 copy-start.27
  155.9 1.3 copy-start.33
  156.7 10.9 %copy-start.6 = (bf16[576,768]{1,0:T(8,128)(2,1)}, bf16[576,768]{1,0:T(8,128)(2,1)S(1)}, u32[]{:S(2)}) copy-start(bf16[576,768]{1,0:T(8,128)(2,1)S(1)} %multiply_convert_fusion.2) | copy-start | bytes 2654212
  156.7 4.2 copy-start.19
  160.9 2.9 copy-start.14
  163.8 26.7 %all-to-all-start.2 = ((bf16[8,152,768]{2,1,0:T(8,128)(2,1)}), bf16[8,152,768]{2,1,0:T(8,128)(2,1)S(1)}, u32[]{:S(2)}, u32[]{:S(2)}) async-start(bf16[8,152,768]{2,1,0:T(8,128)(2,1)} %bitcast.194), calls=%async_computation.2 | async-start | bytes 3735552 | tf_op jit(solution)/shard_map/all_to_all | solution.py:190
  190.5 1.2 copy-start.12
  191.7 27.1 %all-to-all-start = ((bf16[8,152,768]{2,1,0:T(8,128)(2,1)}), bf16[8,152,768]{2,1,0:T(8,128)(2,1)}, u32[]{:S(2)}, u32[]{:S(2)}) async-start(bf16[8,152,768]{2,1,0:T(8,128)(2,1)} %bitcast.191), calls=%async_computation | async-start | bytes 3735552 | tf_op jit(solution)/shard_map/all_to_all | solution.py:163
  196.5 477.2 %reduce-scatter.10.cloned.1.call-start = ((), (), s32[]{:S(2)}) async-start(), calls=%async_computation.14 | async-start | bytes 20054016 | tf_op jit(solution)/shard_map/reduce_scatter | solution.py:114
  372.6 392.4 %reduce-scatter.12.cloned.1.call-start = ((), (), s32[]{:S(2)}) async-start(), calls=%async_computation.15 | async-start | bytes 20054016 | tf_op jit(solution)/shard_map/reduce_scatter | solution.py:117
  414.4 27.0 %all-to-all-start.1 = ((bf16[4,304,768]{2,0,1:T(4,128)(2,1)}), bf16[4,304,768]{2,0,1:T(4,128)(2,1)S(1)}, u32[]{:S(2)}, u32[]{:S(2)}) async-start(bf16[4,304,768]{2,0,1:T(4,128)(2,1)} %copy.108), calls=%async_computation.1 | async-start | bytes 3735552 | tf_op jit(solution)/shard_map/all_to_all | solution.py:165
  435.3 12.2 %copy-start.28 = (s32[576,2]{0,1:T(2,128)S(1)}, s32[576,2]{0,1:T(2,128)}, u32[]{:S(2)}) copy-start(s32[576,2]{0,1:T(2,128)} %get-tuple-element.199) | copy-start | bytes 13828
  441.4 1.2 copy-start.11
  442.6 27.1 %all-to-all-start.3 = ((bf16[4,304,768]{2,0,1:T(4,128)(2,1)}), bf16[4,304,768]{2,0,1:T(4,128)(2,1)}, u32[]{:S(2)}, u32[]{:S(2)}) async-start(bf16[4,304,768]{2,0,1:T(4,128)(2,1)} %copy.112), calls=%async_computation.3 | async-start | bytes 3735552 | tf_op jit(solution)/shard_map/all_to_all | solution.py:194
  447.4 422.2 %reduce-scatter.8.cloned.1.call-start = ((), (), s32[]{:S(2)}) async-start(), calls=%async_computation.13 | async-start | bytes 2433024 | tf_op jit(solution)/shard_map/reduce_scatter | solution.py:226
  482.4 7.1 copy-start.22
  482.4 7.3 copy-start.16
  489.7 3.0 copy-start.1
  492.7 1.2 copy-start.20
  493.8 1.9 copy-start.35
  494.5 1.2 copy-start.3
  503.4 491.0 %reduce-scatter.6.cloned.1.call-start = ((), (), s32[]{:S(2)}) async-start(), calls=%async_computation.12 | async-start | bytes 7299072 | tf_op jit(solution)/shard_map/reduce_scatter | solution.py:225
  604.4 1.5 copy-start.17
  604.4 1.8 copy-start.18
  606.1 2.2 copy-start.9
  606.2 2.2 copy-start.26
  606.2 2.2 copy-start.30
  606.2 2.2 copy-start.32
  606.7 1.7 copy-start.13
  613.8 1.2 copy-start.7
  615.2 52.2 %copy-start.10 = (bf16[576,768]{1,0:T(8,128)(2,1)S(1)}, bf16[576,768]{1,0:T(8,128)(2,1)}, u32[]{:S(2)}) copy-start(bf16[576,768]{1,0:T(8,128)(2,1)} %param.15) | copy-start | bytes 2654212
  667.4 4.0 copy-start.2
  667.4 4.0 copy-start.15
Sparse Core Ops, SparseCore 0:
  10.9 62.6 all-gather.5
  76.6 52.6 all-gather.7
  130.9 97.8 all-gather.11
  230.2 98.8 all-gather.9
  372.7 194.0 reduce-scatter.9
  570.7 194.1 reduce-scatter.11
  770.8 98.7 reduce-scatter.7
  875.8 118.5 reduce-scatter.5
where the time goes:
time: 1010 us; the launch traced here: 1000 us
  waiting for transfers between devices  477 us (47%)
  matrix products  276 us (27%)
  blocking collectives  126 us (12%)
  local copies, waits for them, and re-layouts  66.9 us (7%)
  other arithmetic  22.4 us (2%)
  starting transfers between devices  18.3 us (2%)
  between operations  15.1 us (1%)
    reduce_scatter x1, waiting for transfers between devices, per_device(): lax.psum_scatter(d_qkv, ('dp', 'fsdp'), scatter_dimension=0, tiled=True)  125 us
    reduce_scatter x1, waiting for transfers between devices, per_device(): lax.psum_scatter(d_proj, ('dp', 'fsdp'), scatter_dimension=0, tiled=True)  102 us
    reduce_scatter x1, waiting for transfers between devices, reduce_experts(): lax.psum_scatter(grad_down.astype(jnp.bfloat16), 'fsdp', scatter_dimensio...  88.2 us
    all_gather x1, waiting for transfers between devices, gather_experts(): lax.all_gather(local_pair[0], 'fsdp', axis=1, tiled=True)  87.4 us
    unnamed x2, blocking collectives  85.2 us
    all_gather x1, blocking collectives, gather_dense(): lax.all_gather(w_router, ('dp', 'fsdp'), axis=0, tiled=True)  40.8 us
    dot_general x1, matrix products, expert_forward(): jnp.einsum('ecd,edf->ecf', expert_rows, w_up, preferred_element_type=jnp....  26.9 us
    dot_general x12, matrix products, head_forward(): jnp.einsum('ist,itd->isd', attn_probs, values_head, preferred_element_typ...  23.4 us
  transfers between devices with their start and end apart: 12, of which 9 were waited for; matrix products, arithmetic and copies ran while one was open for 31% of the time, Pallas kernels for 0%

commit v1 on v0

--- a/solution.py
+++ b/solution.py
@@ -9,6 +9,22 @@
 SEQ = 576
 CAP = 152
 norm_epsilon = 1e-06
+
+
+def frames_wait(my_data):
+    a_name = "fsdp"
+    inter = jax.lax.axis_size(a_name)
+    a_next, v_next = (inter, jax.lax.axis_index(a_name))
+    local_now, new = (my_data, 1)
+    while new < a_next:
+        aux = jax.lax.ppermute(
+            local_now, axis_name=a_name, perm=[(dev_i, dev_i ^ new) for dev_i in range(a_next)]
+        )
+        extra = jnp.concatenate([local_now, aux], 1)
+        q_next = jnp.concatenate([aux, local_now], 1)
+        local_now = jnp.where(v_next & new == 0, extra, q_next)
+        new = 2 * new
+    return local_now
 
 
 def norm_parts(values):
@@ -103,10 +119,7 @@
 
 def gather_experts(w_in, w_out):
     local_pair = (w_in, w_out)
-    return (
-        lax.all_gather(local_pair[0], "fsdp", axis=1, tiled=True),
-        lax.all_gather(local_pair[1], "fsdp", axis=1, tiled=True),
-    )
+    return (frames_wait(local_pair[0]), lax.all_gather(local_pair[1], "fsdp", axis=1, tiled=True))
 
 
 def reduce_experts(grad_up, grad_down):

time: 1010 us -> 1430 us (1.42)
  waiting for transfers between devices: 477 us -> 725 us
  blocking collectives: 126 us -> 265 us
  other arithmetic: 22.4 us -> 43.9 us
    ppermute x0 -> x4, waiting for transfers between devices: none -> 347 us  [frames_wait(): jax.lax.ppermute(local_now, axis_name=a_name, perm=[(dev_i, dev_i ^ new)...]
    unnamed x2, blocking collectives: 85.2 us -> 225 us
    all_gather x1 -> x0, waiting for transfers between devices: 87.4 us -> none  [gather_experts(): lax.all_gather(local_pair[0], 'fsdp', axis=1, tiled=True)]
    select_n x0 -> x3, other arithmetic: none -> 21.5 us  [frames_wait(): local_now = jnp.where(v_next & new == 0, extra, q_next)]
  transfers between devices with their start and end apart: 12 -> 15, of which waited for: 9 -> 10; matrix products, arithmetic and copies ran while one was open for 31% -> 24% of each run, Pallas kernels for 0% -> 0%
where the time goes in v1:
time: 1430 us; the launch traced here: 1420 us
  waiting for transfers between devices  725 us (51%)
  matrix products  282 us (20%)
  blocking collectives  265 us (19%)
  local copies, waits for them, and re-layouts  66.1 us (5%)
  other arithmetic  43.9 us (3%)
  starting transfers between devices  23.6 us (2%)
  between operations  15.3 us (1%)
    ppermute x4, waiting for transfers between devices, frames_wait(): jax.lax.ppermute(local_now, axis_name=a_name, perm=[(dev_i, dev_i ^ new)...  347 us
    unnamed x2, blocking collectives  225 us
    reduce_scatter x1, waiting for transfers between devices, per_device(): lax.psum_scatter(d_qkv, ('dp', 'fsdp'), scatter_dimension=0, tiled=True)  125 us
    reduce_scatter x1, waiting for transfers between devices, per_device(): lax.psum_scatter(d_proj, ('dp', 'fsdp'), scatter_dimension=0, tiled=True)  102 us
    reduce_scatter x1, waiting for transfers between devices, reduce_experts(): lax.psum_scatter(grad_down.astype(jnp.bfloat16), 'fsdp', scatter_dimensio...  89.5 us
    all_gather x1, blocking collectives, gather_dense(): lax.all_gather(w_router, ('dp', 'fsdp'), axis=0, tiled=True)  40.6 us
    dot_general x1, matrix products, expert_forward(): jnp.einsum('ecd,edf->ecf', expert_rows, w_up, preferred_element_type=jnp....  29.3 us
  transfers between devices with their start and end apart: 15, of which 10 were waited for; matrix products, arithmetic and copies ran while one was open for 24% of the time, Pallas kernels for 0%

profile of v1, /device:TPU:0, one launch (start us, length us, event | category | flops | bytes accessed | tf_op | source)
XLA Modules:
  0.0 1421.8 jit_solution(14740128246822833826)
XLA Ops:
  10.0 2.8 collective-permute-done
  12.8 2.4 maximum_select_fusion.5
  15.2 2.9 collective-permute-start.1
  18.1 60.3 %collective-permute-done.1 = bf16[4,96,3072]{2,1,0:T(8,128)(2,1)} collective-permute-done((bf16[4,96,3072]{2,1,0:T(8,128)(2,1)S(1)}, bf16[4,96,3072]{2,1,0:T(8,128)(2,1)}, u32[]{:S(2)}, u32[]{:S(2)}) %collective-permute-start.1) | collective-permute-done | bytes 2359328 | tf_op jit(solution)/shard_map/ppermute | solution.py:20
  78.5 6.6 maximum_select_fusion.2
  87.3 182.6 %all-reduce.6 = (bf16[768]{0:T(1024)(128)(2,1)S(1)}, bf16[768]{0:T(1024)(128)(2,1)S(1)}) all-reduce(bf16[768]{0:T(1024)(128)(2,1)S(1)} %dynamic-update-slice, bf16[768]{0:T(1024)(128)(2,1)S(1)} %dynamic-update-slice.1), channel_id=1, replica_groups=mesh['dp'=2,'fsdp'=16] {'dp','fsdp'}, use_global_device_ids=true, to_apply=%add | all-reduce | flops 1536 | bytes 6144
  269.9 40.6 %all-gather = bf16[32,24,8]{1,2,0:T(8,128)(2,1)S(1)} all-gather(bf16[1,24,8]{1,2,0:T(8,128)(2,1)S(1)} %bitcast.197), channel_id=1, replica_groups=mesh['dp'=2,'fsdp'=16] {'dp','fsdp'}, dimensions={0}, use_global_device_ids=true | all-gather | bytes 12672 | tf_op jit(solution)/shard_map/all_gather | solution.py:116
  312.5 5.9 convolution_convert_fusion.3
  318.4 4.0 copy.102
  328.0 2.6 copy.105
  330.5 12.5 maximum_select_fusion.1
  343.1 37.7 %while.26 = (s32[]{:T(128)}, bf16[12,1,576,64]{2,3,1,0:T(8,128)(2,1)}, f32[12,1,576]{2,1,0:T(1,128)}, bf16[12,1,576,64]{3,2,1,0:T(8,128)(2,1)S(1)}, bf16[12,1,57...) while((s32[]{:T(128)}, bf16[12,1,576,64]{2,3,1,0:T(8,128)(2,1)}, ...), condition=%wide.region_5.6_spmd, body=%wide.region_2.5_spmd.sunk | while | flops 87293376 | bytes 4531033 | solution.py:150
  343.7 1.9 fusion.137
  346.9 1.9 fusion.137
  350.0 1.9 fusion.137
  353.1 1.9 fusion.137
  356.3 1.9 fusion.137
  359.4 1.9 fusion.137
  362.6 1.9 fusion.137
  365.7 1.9 fusion.137
  368.9 1.9 fusion.137
  372.0 1.9 fusion.137
  375.1 1.9 fusion.137
  378.3 1.9 fusion.137
  380.8 4.1 fusion.80
  387.1 3.7 fusion.50
  390.9 2.9 convolution_convert_fusion.4
  393.8 4.1 all-to-all-start.2
  397.9 4.3 convolution_convert_fusion.5
  402.2 18.8 %all-to-all-done.2 = bf16[8,152,768]{2,1,0:T(8,128)(2,1)S(1)} async-done(((bf16[8,152,768]{2,1,0:T(8,128)(2,1)}), bf16[8,152,768]{2,1,0:T(8,128)(2,1)S(1)}, u32[]{:S(2)}, u32[]{:S(2)}) %all-to-all-start.2) | async-done | bytes 1867808 | tf_op jit(solution)/shard_map/all_to_all | solution.py:203
  422.3 4.7 all-to-all-start
  428.7 20.8 %all-to-all-done = bf16[8,152,768]{2,1,0:T(8,128)(2,1)} async-done(((bf16[8,152,768]{2,1,0:T(8,128)(2,1)}), bf16[8,152,768]{2,1,0:T(8,128)(2,1)}, u32[]{:S(2)}, u32[]{:S(2)}) %all-to-all-start) | async-done | bytes 1867808 | tf_op jit(solution)/shard_map/all_to_all | solution.py:176
  449.5 2.9 copy.107
  452.4 12.8 fusion.82
  465.2 283.8 %collective-permute-done.3 = bf16[4,384,3072]{2,1,0:T(8,128)(2,1)} collective-permute-done((bf16[4,384,3072]{2,1,0:T(8,128)(2,1)}, bf16[4,384,3072]{2,1,0:T(8,128)(2,1)}, u32[]{:S(2)}, u32[]{:S(2)}) %collective-permute-start.3) | collective-permute-done | bytes 9437216 | tf_op jit(solution)/shard_map/ppermute | solution.py:20
  749.0 29.3 %fusion.43 = (bf16[4,304,3072]{2,1,0:T(8,128)(2,1)}, f32[4,304,3072]{2,1,0:T(8,128)}) fusion(f32[4,304,3072]{2,1,0:T(8,128)} %fusion.82, bf16[4,304,768]{2,1,0:T(8,128)(2,1)} %bitcast.190, bf16[4,384,3072]{2,1,0:T(8,128)(2,1)} %collective-permute-done.3, bf16[4,384,3072]{2,1,0:T(8,128)(2,1)} %maximum_select_fusion.1, pred[]{:T(512)S(6)} %eq.48), kind=kOutput, calls=%fused_computation.60 | convolution fusion | flops 5897453568 | bytes 58097664 | tf_op jit(solution)/shard_map/ecd,edf->ecf/dot_general | solution.py:88
  778.3 16.7 %convolution_convert_fusion.2 = bf16[4,768,3072]{2,1,0:T(8,128)(2,1)} fusion(bf16[4,304,768]{2,1,0:T(8,128)(2,1)} %bitcast.191, bf16[4,304,3072]{2,1,0:T(8,128)(2,1)} %get-tuple-element.212), kind=kOutput, calls=%fused_computation.63 | convolution fusion | flops 5747245056 | bytes 28213248 | tf_op jit(solution)/shard_map/ecd,ecf->edf/dot_general | solution.py:103
  795.2 20.1 %convolution_convert_fusion.1 = bf16[4,3072,768]{2,1,0:T(8,128)(2,1)} fusion(bf16[4,304,768]{2,1,0:T(8,128)(2,1)S(1)} %bitcast.181, f32[4,304,3072]{2,1,0:T(8,128)} %get-tuple-element.213), kind=kOutput, calls=%fused_computation.62 | convolution fusion | flops 5780865024 | bytes 35684352 | tf_op jit(solution)/shard_map/ecf,ecd->efd/dot_general | solution.py:102
  815.4 18.4 %convolution_convert_fusion.6 = bf16[4,304,768]{2,1,0:T(8,128)(2,1)S(1)} fusion(bf16[4,3072,768]{2,1,0:T(8,128)(2,1)} %all-gather.9.cloned.1.call-done, f32[4,304,3072]{2,1,0:T(8,128)} %get-tuple-element.213), kind=kOutput, calls=%fused_computation.91 | convolution fusion | flops 5772361728 | bytes 35684352 | tf_op jit(solution)/shard_map/ecf,efd->ecd/dot_general | solution.py:90
  833.8 2.2 copy.108
  836.0 3.9 all-to-all-start.1
  839.9 18.3 %fusion.57 = bf16[4,304,768]{2,1,0:T(8,128)(2,1)} fusion(bf16[4,304,3072]{2,1,0:T(8,128)(2,1)} %get-tuple-element.212, bf16[4,384,3072]{2,1,0:T(8,128)(2,1)} %collective-permute-done.3, bf16[4,384,3072]{2,1,0:T(8,128)(2,1)} %maximum_select_fusion.1, pred[]{:T(512)S(6)} %eq.48), kind=kOutput, calls=%fused_computation.90 | convolution fusion | flops 5823676416 | bytes 28213248 | tf_op jit(solution)/shard_map/ecf,edf->ecd/dot_general | solution.py:104
  858.2 3.7 copy.112
  862.8 4.8 all-to-all-start.3
  869.9 20.0 %all-to-all-done.3 = bf16[4,304,768]{2,0,1:T(4,128)(2,1)} async-done(((bf16[4,304,768]{2,0,1:T(4,128)(2,1)}), bf16[4,304,768]{2,0,1:T(4,128)(2,1)}, u32[]{:S(2)}, u32[]{:S(2)}) %all-to-all-start.3) | async-done | bytes 1867808 | tf_op jit(solution)/shard_map/all_to_all | solution.py:207
  892.9 4.8 gather_fusion
  897.8 4.7 reshape.217
  902.5 6.0 fusion.65
  909.8 2.9 fusion.83
  919.3 4.3 fusion.69
  923.9 100.6 %while.27 = (s32[]{:T(128)}, bf16[12,1,576,64]{2,3,1,0:T(8,128)(2,1)}, bf16[12,1,576,64]{2,3,1,0:T(8,128)(2,1)}, bf16[12,1,576,64]{2,3,1,0:T(8,128)(2,1)}, bf16[...) while((s32[]{:T(128)}, ...), condition=%wide.region_19.20_spmd, body=%wide.region_17.19_spmd.sunk | while | flops 215064000 | bytes 11510129 | solution.py:221
  946.1 1.9 fusion.148
  1004.5 2.0 fusion.148
  1013.1 1.9 fusion.148
  1028.4 5.5 fusion.76
  1035.2 7.2 fusion.63
  1042.5 42.1 %all-reduce.5 = (f32[768]{0:T(1024)S(1)}, f32[768]{0:T(1024)S(1)}, f32[768,8]{0,1:T(8,128)S(1)}) all-reduce(f32[768]{0:T(1024)S(1)} %get-tuple-element.158, f32[768]{0:T(1024)S(1)} %get-tuple-element.156, f32[768,8]{0,1:T(8,128)S(1)} %fusion.84), channel_id=2, replica_groups=mesh['dp'=2,'fsdp'=16] {'dp','fsdp'}, use_global_device_ids=true, to_apply=%region_23.24.clone | all-reduce | flops 7680 | bytes 61440
  1086.5 4.0 fusion.62
  1090.5 2.2 add_convert_fusion
  1092.7 2.9 convert_element_type.122
  1095.7 89.5 %reduce-scatter.12.cloned.1.call-done = bf16[4,192,768]{2,1,0:T(8,128)(2,1)} async-done(((bf16[4,3072,768]{2,1,0:T(8,128)(2,1)}), bf16[4,192,768]{2,1,0:T(8,128)(2,1)}) %reduce-scatter.12.cloned.1.call-update) | async-done | bytes 1179664 | tf_op jit(solution)/shard_map/reduce_scatter | solution.py:130
  1185.1 2.9 convert_element_type.124
  1188.0 101.6 %reduce-scatter.8.cloned.1.call-done = f32[24,768]{1,0:T(8,128)} async-done(((f32[768,768]{1,0:T(8,128)}), f32[24,768]{1,0:T(8,128)}) %reduce-scatter.8.cloned.1.call-update) | async-done | bytes 73744 | tf_op jit(solution)/shard_map/reduce_scatter | solution.py:239
  1289.6 124.9 %reduce-scatter.6.cloned.1.call-done = f32[24,2304]{1,0:T(8,128)} async-done(((f32[768,2304]{1,0:T(8,128)}), f32[24,2304]{1,0:T(8,128)}) %reduce-scatter.6.cloned.1.call-update) | async-done | bytes 221200 | tf_op jit(solution)/shard_map/reduce_scatter | solution.py:238
  (316 shorter events, 147.9 us)
Async XLA Ops:
  7.2 5.6 copy-start.17
  7.2 305.3 %all-gather.5.cloned.1.call-start = ((), (), s32[]{:S(2)}) async-start(), calls=%async_computation.8 | async-start | bytes 3649536 | tf_op jit(solution)/shard_map/all_gather | solution.py:113
  7.9 372.9 %all-gather.7.cloned.1.call-start = ((), (), s32[]{:S(2)}) async-start(), calls=%async_computation.9 | async-start | bytes 1216512 | tf_op jit(solution)/shard_map/all_gather | solution.py:114
  8.7 443.7 %all-gather.9.cloned.1.call-start = ((), (), s32[]{:S(2)}) async-start(), calls=%async_computation.10 | async-start | bytes 20054016 | tf_op jit(solution)/shard_map/all_gather | solution.py:122
  9.4 3.4 collective-permute-start
  15.2 63.3 %collective-permute-start.1 = (bf16[4,96,3072]{2,1,0:T(8,128)(2,1)S(1)}, bf16[4,96,3072]{2,1,0:T(8,128)(2,1)}, u32[]{:S(2)}, u32[]{:S(2)}) collective-permute-start(bf16[4,96,3072]{2,1,0:T(8,128)(2,1)S(1)} %maximum_select_fusion.5), channel_id=1, source_target_pairs={{0,2},{1,3},{2,0},{3,1},{4,6},{5,7},{6,4},{7,5},{8,10},{9,11},{10,... | collective-permute-start | bytes 7077896 | tf_op jit(solution)/shard_map/ppermute | solution.py:20
  18.1 68.8 %copy-start.52 = (bf16[24]{0:T(256)(128)(2,1)S(1)}, bf16[24]{0:T(256)(128)(2,1)}, u32[]{:S(2)}) copy-start(bf16[24]{0:T(256)(128)(2,1)} %param.16) | copy-start | bytes 148
  18.1 69.0 %copy-start.53 = (bf16[24]{0:T(256)(128)(2,1)S(1)}, bf16[24]{0:T(256)(128)(2,1)}, u32[]{:S(2)}) copy-start(bf16[24]{0:T(256)(128)(2,1)} %param.19) | copy-start | bytes 148
  18.1 251.8 %copy-start.50 = (bf16[24,8]{0,1:T(8,128)(2,1)S(1)}, bf16[24,8]{0,1:T(8,128)(2,1)}, u32[]{:S(2)}) copy-start(bf16[24,8]{0,1:T(8,128)(2,1)} %param.20) | copy-start | bytes 1156
  18.1 292.5 %copy-start.8 = (bf16[576,768]{1,0:T(8,128)(2,1)S(1)}, bf16[576,768]{1,0:T(8,128)(2,1)}, u32[]{:S(2)}) copy-start(bf16[576,768]{1,0:T(8,128)(2,1)} %param.15) | copy-start | bytes 2654212
  85.1 226.2 %copy-start.36 = (s32[576,2]{0,1:T(2,128)S(1)}, s32[576,2]{0,1:T(2,128)}, u32[]{:S(2)}) copy-start(s32[576,2]{0,1:T(2,128)} %param.24) | copy-start | bytes 13828
  85.1 226.8 %copy-start.38 = (s32[576,2]{0,1:T(2,128)S(1)}, s32[576,2]{0,1:T(2,128)}, u32[]{:S(2)}) copy-start(s32[576,2]{0,1:T(2,128)} %param.23) | copy-start | bytes 13828
  85.1 245.5 %collective-permute-start.2 = (bf16[4,192,3072]{2,1,0:T(8,128)(2,1)}, bf16[4,192,3072]{2,1,0:T(8,128)(2,1)}, u32[]{:S(2)}, u32[]{:S(2)}) collective-permute-start(bf16[4,192,3072]{2,1,0:T(8,128)(2,1)} %maximum_select_fusion.2), channel_id=1, source_target_pairs={{0,4},{1,5},{2,6},{3,7},{4,0},{5,1},{6,2},{7,3},{8,12},{9,13},{10,... | collective-permute-start | bytes 14155784 | tf_op jit(solution)/shard_map/ppermute | solution.py:20
  269.9 48.5 %copy-start.45 = (f32[768]{0:T(1024)}, f32[768]{0:T(1024)S(1)}, u32[]{:S(2)}) copy-start(f32[768]{0:T(1024)S(1)} %convert_element_type.101) | copy-start | bytes 9220
  269.9 115.4 %copy-start.32 = (f32[768]{0:T(1024)}, f32[768]{0:T(1024)S(1)}, u32[]{:S(2)}) copy-start(f32[768]{0:T(1024)S(1)} %convert_element_type.104) | copy-start | bytes 9220
  310.6 75.3 %copy-start.24 = (bf16[768,8]{0,1:T(8,128)(2,1)}, bf16[768,8]{0,1:T(8,128)(2,1)S(1)}, u32[]{:S(2)}) copy-start(bf16[768,8]{0,1:T(8,128)(2,1)S(1)} %reshape.231) | copy-start | bytes 36868
  310.9 7.5 copy-start.41
  311.9 6.5 copy-start.47
  343.1 405.9 %collective-permute-start.3 = (bf16[4,384,3072]{2,1,0:T(8,128)(2,1)}, bf16[4,384,3072]{2,1,0:T(8,128)(2,1)}, u32[]{:S(2)}, u32[]{:S(2)}) collective-permute-start(bf16[4,384,3072]{2,1,0:T(8,128)(2,1)} %maximum_select_fusion.1), channel_id=1, source_target_pairs={{0,8},{1,9},{2,10},{3,11},{4,12},{5,13},{6,14},{7,15},{8,0},{9,1},... | collective-permute-start | bytes 28311560 | tf_op jit(solution)/shard_map/ppermute | solution.py:20
  380.8 4.1 copy-start.4
  380.8 4.1 copy-start.5
  384.9 1.2 copy-start
  385.3 1.3 copy-start.39
  385.3 1.8 copy-start.43
  385.3 1.8 copy-start.49
  385.6 5.2 copy-start.34
  386.1 11.8 copy-start.6
  386.2 4.7 copy-start.20
  386.5 7.3 copy-start.26
  390.9 2.9 copy-start.14
  393.8 27.2 %all-to-all-start.2 = ((bf16[8,152,768]{2,1,0:T(8,128)(2,1)}), bf16[8,152,768]{2,1,0:T(8,128)(2,1)S(1)}, u32[]{:S(2)}, u32[]{:S(2)}) async-start(bf16[8,152,768]{2,1,0:T(8,128)(2,1)} %bitcast.192), calls=%async_computation.2 | async-start | bytes 3735552 | tf_op jit(solution)/shard_map/all_to_all | solution.py:203
  421.0 1.2 copy-start.12
  422.3 27.2 %all-to-all-start = ((bf16[8,152,768]{2,1,0:T(8,128)(2,1)}), bf16[8,152,768]{2,1,0:T(8,128)(2,1)}, u32[]{:S(2)}, u32[]{:S(2)}) async-start(bf16[8,152,768]{2,1,0:T(8,128)(2,1)} %bitcast.189), calls=%async_computation | async-start | bytes 3735552 | tf_op jit(solution)/shard_map/all_to_all | solution.py:176
  427.0 665.7 %reduce-scatter.10.cloned.1.call-start = ((), (), s32[]{:S(2)}) async-start(), calls=%async_computation.13 | async-start | bytes 20054016 | tf_op jit(solution)/shard_map/reduce_scatter | solution.py:127
  795.0 390.1 %reduce-scatter.12.cloned.1.call-start = ((), (), s32[]{:S(2)}) async-start(), calls=%async_computation.14 | async-start | bytes 20054016 | tf_op jit(solution)/shard_map/reduce_scatter | solution.py:130
  836.0 26.8 %all-to-all-start.1 = ((bf16[4,304,768]{2,0,1:T(4,128)(2,1)}), bf16[4,304,768]{2,0,1:T(4,128)(2,1)S(1)}, u32[]{:S(2)}, u32[]{:S(2)}) async-start(bf16[4,304,768]{2,0,1:T(4,128)(2,1)} %copy.108), calls=%async_computation.1 | async-start | bytes 3735552 | tf_op jit(solution)/shard_map/all_to_all | solution.py:178
  861.9 5.7 copy-start.44
  862.8 4.9 copy-start.11
  862.8 27.0 %all-to-all-start.3 = ((bf16[4,304,768]{2,0,1:T(4,128)(2,1)}), bf16[4,304,768]{2,0,1:T(4,128)(2,1)}, u32[]{:S(2)}, u32[]{:S(2)}) async-start(bf16[4,304,768]{2,0,1:T(4,128)(2,1)} %copy.112), calls=%async_computation.3 | async-start | bytes 3735552 | tf_op jit(solution)/shard_map/all_to_all | solution.py:207
  867.6 422.0 %reduce-scatter.8.cloned.1.call-start = ((), (), s32[]{:S(2)}) async-start(), calls=%async_computation.12 | async-start | bytes 2433024 | tf_op jit(solution)/shard_map/reduce_scatter | solution.py:239
  902.4 7.2 copy-start.37
  902.4 7.2 copy-start.40
  902.4 7.2 copy-start.23
  902.4 7.3 copy-start.27
  902.5 7.3 copy-start.31
  902.5 7.3 copy-start.16
  909.8 3.0 copy-start.1
  909.8 3.0 copy-start.25
  909.8 3.0 copy-start.29
  909.8 3.0 copy-start.33
  909.8 3.0 copy-start.35
  914.0 1.9 copy-start.51
  914.7 1.2 copy-start.3
  923.6 490.9 %reduce-scatter.6.cloned.1.call-start = ((), (), s32[]{:S(2)}) async-start(), calls=%async_computation.11 | async-start | bytes 7299072 | tf_op jit(solution)/shard_map/reduce_scatter | solution.py:238
  1024.5 1.5 copy-start.18
  1024.5 1.8 copy-start.19
  1026.3 2.2 copy-start.9
  1026.3 2.2 copy-start.42
  1026.3 2.2 copy-start.46
  1026.3 2.2 copy-start.48
  1026.8 1.6 copy-start.13
  1035.2 51.2 %copy-start.10 = (bf16[576,768]{1,0:T(8,128)(2,1)S(1)}, bf16[576,768]{1,0:T(8,128)(2,1)}, u32[]{:S(2)}) copy-start(bf16[576,768]{1,0:T(8,128)(2,1)} %param.15) | copy-start | bytes 2654212
  1086.4 4.0 copy-start.2
  1086.4 4.0 copy-start.15
  (5 other events, 4.2 us)
Sparse Core Ops, SparseCore 0:
  10.9 68.8 all-gather.4
  82.7 53.3 all-gather.6
  137.7 147.9 all-gather.8
  795.1 191.7 reduce-scatter.9
  990.9 194.2 reduce-scatter.11
  1190.8 98.6 reduce-scatter.7
  1295.8 118.6 reduce-scatter.5
